TPU v7x, 32 devices: a whole 2x2x4 slice. The times are simulated.
32 devices in a mesh: row: 4 (over z), col: 8 (over y, x, core).
Axes of the slice: x: 2, y: 2, z: 4, core: 2. Of those that a mesh axis runs over, the one named last changes fastest.
Arguments:
- matrix_tiles: float32 [4, 8, 16, 512, 512], P('row', 'col'), may hold values from -0.25 to 0.25
- tile_rows: int32 [4, 8, 16], P('row', 'col'), may hold values from 0 to 63, as said below
- tile_columns: int32 [4, 8, 16], P('row', 'col'), may hold values from 0 to 31, as said below
- tile_counts: int32 [4, 8], P('row', 'col'), may hold values from 8 to 16, as said below
- primal_iter: float32 [2, 131072], P(None, ('col', 'row')), may hold values from -6 to 6
- dual_iter: float32 [2, 131072], P(None, ('row', 'col')), may hold values from -6 to 6
- requirement: float32 [131072], P('row'), may hold values from -68 to 68
- constraint_kind: int32 [131072], P('row'), may hold values from 0 to 1
- objective: float32 [131072], P('col'), may hold values from -68 to 68
- lower_bound: float32 [131072], P('col'), may hold values from -1.5 to 1.5
- upper_bound: float32 [131072], P('col'), may hold values from -1.5 to 1.5
- variable_kind: int32 [131072], P('col'), may hold values from 0 to 3
Outputs:
- primal_residual: float32 [2, 131072], P(None, ('row', 'col'))
- dual_residual: float32 [2, 131072], P(None, ('col', 'row'))
- metrics: float32 [2, 3], replicated
Inputs may be any that keep to these rules, and one draw needn't show every extreme that they name: `tile_counts`: slots below the count of a list hold live tiles, the others are padding; some list has all 16 slots live. `tile_rows`: in each constraint group, the first (8) slots of its lists name every block row of the group exactly once; later slots name any block row, and repeated tiles add. `tile_columns`: in each variable group, the first (8) slots of its lists name every block column of the group exactly once; later slots name any block column, and repeated tiles add. `constraint_kind`: 0 marks an equality, 1 a constraint of the form at least. `variable_kind`: 0 free, 1 lower bound only, 2 upper bound only, 3 both bounds.
All inputs are finite; a program needn't handle non-finite values.
Results may differ from a plain program's by a relative error of at most 0.0003.
Values sent between devices are 32-bit elements; how exact they have to be, the bound alone decides.
No kernel may reach another device: no remote copies, remote signals or barrier semaphores. Data moves between devices by JAX's collectives and lax.ppermute only.
A program may use at most 64 MiB of HBM per device.

v0:
```python
import jax
import jax.numpy as jnp
from jax import lax
from jax.sharding import PartitionSpec as P

HIGHEST_PRECISION = lax.Precision.HIGHEST


def primal_side(product, require_part, kind_part, dual_part):
    difference = require_part[None, :] - product
    residual = jnp.where(kind_part[None, :] == 1, jnp.maximum(difference, 0.0), difference)
    return (
        residual,
        jnp.sum(residual * residual, axis=1),
        jnp.sum(require_part * require_part),
        jnp.sum(require_part[None, :] * dual_part, axis=1),
    )


def dual_side(transposed, objective, lower_bound, upper_bound, variable_kind, primal_part):
    reduced = objective[None, :] - transposed
    lower_active = (variable_kind == 1) | (variable_kind == 3)
    upper_active = (variable_kind == 2) | (variable_kind == 3)
    multiplier = jnp.where(lower_active[None, :], jnp.maximum(reduced, 0.0), 0.0) + jnp.where(
        upper_active[None, :], jnp.minimum(reduced, 0.0), 0.0
    )
    residual = reduced - multiplier
    bound_sum = jnp.sum(
        lower_bound[None, :] * jnp.maximum(multiplier, 0.0)
        + upper_bound[None, :] * jnp.minimum(multiplier, 0.0),
        axis=1,
    )
    return (
        residual,
        jnp.sum(residual * residual, axis=1),
        jnp.sum(objective * objective),
        jnp.sum(objective[None, :] * primal_part, axis=1),
        bound_sum,
    )


def finish(
    primal_square,
    require_square,
    require_dot,
    dual_square,
    objective_square,
    objective_dot,
    bound_sum,
):
    primal_ratio = jnp.sqrt(primal_square) / (1.0 + jnp.sqrt(require_square))
    dual_ratio = jnp.sqrt(dual_square) / (1.0 + jnp.sqrt(objective_square))
    dual_value = require_dot + bound_sum
    duality_gap = jnp.abs(objective_dot - dual_value) / (
        1.0 + jnp.abs(objective_dot) + jnp.abs(dual_value)
    )
    return jnp.stack([primal_ratio, dual_ratio, duality_gap], axis=1)


def on_device(
    matrix_tiles,
    tile_rows,
    tile_columns,
    tile_counts,
    primal_iter,
    dual_iter,
    requirement,
    constraint_kind,
    objective,
    lower_bound,
    upper_bound,
    variable_kind,
):
    own_tiles = matrix_tiles[0, 0]
    slot_count = own_tiles.shape[0]
    block_size = own_tiles.shape[-1]
    candidates = primal_iter.shape[0]
    active = (lax.iota(jnp.int32, slot_count) < tile_counts[0, 0]).astype(jnp.float32)
    primal_group = lax.all_gather(primal_iter, "row", axis=1, tiled=True)
    dual_group = lax.all_gather(dual_iter, "col", axis=1, tiled=True)
    column_blocks = primal_group.shape[1] // block_size
    row_blocks = dual_group.shape[1] // block_size
    column_pick = (
        tile_columns[0, 0][:, None] == lax.iota(jnp.int32, column_blocks)[None, :]
    ).astype(jnp.float32)
    column_pick = column_pick * active[:, None]
    row_pick = (tile_rows[0, 0][:, None] == lax.iota(jnp.int32, row_blocks)[None, :]).astype(
        jnp.float32
    )
    row_pick = row_pick * active[:, None]
    primal_pick = jnp.einsum(
        "tc,scb->stb",
        column_pick,
        primal_group.reshape(candidates, column_blocks, block_size),
        precision=HIGHEST_PRECISION,
    )
    dual_pick = jnp.einsum(
        "tr,srb->stb",
        row_pick,
        dual_group.reshape(candidates, row_blocks, block_size),
        precision=HIGHEST_PRECISION,
    )
    tile_product = jnp.einsum("tij,stj->tsi", own_tiles, primal_pick, precision=HIGHEST_PRECISION)
    tile_transposed = jnp.einsum("tij,sti->tsj", own_tiles, dual_pick, precision=HIGHEST_PRECISION)
    row_share = dual_iter.shape[1]
    column_share = primal_iter.shape[1]
    row_start = lax.axis_index("col") * row_share
    column_start = lax.axis_index("row") * column_share
    product_part = jnp.einsum(
        "tr,tsi->sri", row_pick, tile_product, precision=HIGHEST_PRECISION
    ).reshape(candidates, row_blocks * block_size)
    transposed_part = jnp.einsum(
        "tc,tsj->scj", column_pick, tile_transposed, precision=HIGHEST_PRECISION
    ).reshape(candidates, column_blocks * block_size)
    product = lax.psum(product_part, "col")
    transposed = lax.psum(transposed_part, "row")
    primal_full, primal_square, require_square, require_dot = primal_side(
        product, requirement, constraint_kind, dual_group
    )
    primal_square, require_square, require_dot = lax.psum(
        (primal_square, require_square, require_dot), "row"
    )
    dual_full, dual_square, objective_square, objective_dot, bound_sum = dual_side(
        transposed, objective, lower_bound, upper_bound, variable_kind, primal_group
    )
    dual_square, objective_square, objective_dot, bound_sum = lax.psum(
        (dual_square, objective_square, objective_dot, bound_sum), "col"
    )
    primal_residual = lax.dynamic_slice_in_dim(primal_full, row_start, row_share, 1)
    dual_residual = lax.dynamic_slice_in_dim(dual_full, column_start, column_share, 1)
    metrics = finish(
        primal_square,
        require_square,
        require_dot,
        dual_square,
        objective_square,
        objective_dot,
        bound_sum,
    )
    return (primal_residual, dual_residual, metrics)


def solution(mesh):
    placed = (
        P("row", "col", None, None, None),
        P("row", "col", None),
        P("row", "col", None),
        P("row", "col"),
        P(None, ("col", "row")),
        P(None, ("row", "col")),
        P("row"),
        P("row"),
        P("col"),
        P("col"),
        P("col"),
        P("col"),
    )
    return jax.shard_map(
        on_device,
        mesh=mesh,
        in_specs=placed,
        out_specs=(P(None, ("row", "col")), P(None, ("col", "row")), P()),
        check_vma=False,
    )
```

profile of v0, /device:TPU:0, one launch (start us, length us, event | category | flops | bytes accessed | tf_op | source)
XLA Modules:
  0.0 147.8 jit_solution(15917342106605868104)
XLA Ops:
  7.2 0.0 all-reduce.7.cloned.1.call-start
  7.9 11.0 %all_gather.7 = f32[2,32768]{1,0:T(2,128)S(1)} all-gather(f32[2,4096]{1,0:T(2,128)} %param.17), channel_id=1, replica_groups=mesh['row'=4,'col'=8] {'col'}, dimensions={1}, use_global_device_ids=true | all-gather | bytes 294912 | tf_op jit(solution)/shard_map/all_gather | solution.py:80
  18.9 0.9 fusion.4
  19.8 0.0 copy-start.8
  19.8 0.0 copy-start.3
  19.9 0.0 copy-start.1
  19.9 0.0 copy-start.2
  19.9 0.0 copy-start
  19.9 0.0 copy-start.4
  19.9 0.0 copy-start.5
  19.9 11.6 %fusion = f32[16,2,512]{2,1,0:T(2,128)S(1)} fusion(f32[1,1,16,512,512]{4,3,2,1,0:T(8,128)} %param.12, f32[16,2,512]{2,0,1:T(8,128)S(1)} %fusion.4), kind=kOutput, calls=%fused_computation | convolution fusion | flops 100663296 | bytes 16908288 | tf_op jit(solution)/shard_map/tij,sti->tsj/dot_general | solution.py:104
  31.6 0.4 convolution_bitcast_fusion.1
  31.9 0.7 copy.23
  32.7 0.0 all-reduce.7.cloned.1.call-update
  32.7 0.0 all-reduce.5.cloned.1.call-start
  32.8 13.9 %all_gather.6 = f32[2,16384]{1,0:T(2,128)S(1)} all-gather(f32[2,4096]{1,0:T(2,128)S(1)} %copy-done.6), channel_id=1, replica_groups=mesh['row'=4,'col'=8] {'row'}, dimensions={1}, use_global_device_ids=true | all-gather | bytes 163840 | tf_op jit(solution)/shard_map/all_gather | solution.py:79
  46.7 0.3 fusion.7
  46.9 17.2 %fusion.2 = f32[16,2,512]{2,1,0:T(2,128)S(1)} fusion(f32[1,1,16,512,512]{4,3,2,1,0:T(8,128)} %param.12, f32[16,2,512]{2,0,1:T(8,128)S(1)} %fusion.7), kind=kOutput, calls=%fused_computation.2 | convolution fusion | flops 100663296 | bytes 16908288 | tf_op jit(solution)/shard_map/tij,stj->tsi/dot_general | solution.py:103
  64.1 0.5 convolution_bitcast_fusion
  64.6 0.9 copy.21
  65.5 0.0 all-reduce.5.cloned.1.call-update
  65.6 0.6 multiply_reduce_fusion.5
  66.3 0.6 multiply_reduce_fusion.4
  66.9 1.0 all-reduce.7.cloned.1.call-done
  67.9 1.5 add_reduce_fusion
  69.4 12.5 %all-reduce = (f32[2]{0:T(128)S(1)}, f32[2]{0:T(128)S(1)}, f32[2]{0:T(128)S(1)}, f32[]{:T(128)}) all-reduce(f32[2]{0:T(128)S(1)} %get-tuple-element.7, f32[2]{0:T(128)S(1)} %get-tuple-element.6, f32[2]{0:T(128)S(1)} %get-tuple-element.19, f32[]{:T(128)} %multiply_reduce_fusion.5), channel_id=1, replica_groups=mesh['row'=4,'col'=8] {'col'}, use_global_device_ids=true, to_apply=%region_11.12 | all-reduce | flops 7 | bytes 56 | tf_op jit(solution)/shard_map/psum | solution.py:126
  82.6 41.9 %all-reduce.5.cloned.1.call-done = f32[2,32768]{1,0:T(2,128)} async-done(((f32[2,32768]{1,0:T(2,128)}), f32[2,32768]{1,0:T(2,128)}) %all-reduce.5.cloned.1.call-update) | async-done | bytes 262160 | tf_op jit(solution)/shard_map/psum | solution.py:115
  124.5 1.5 %multiply_reduce_fusion.1 = (f32[2]{0:T(128)S(1)}, f32[2,32768]{1,0:T(2,128)S(1)}, f32[2]{0:T(128)S(1)}) fusion(f32[2,32768]{1,0:T(2,128)} %all-reduce.5.cloned.1.call-done, f32[32768]{0:T(1024)S(1)} %copy-done, pred[32768]{0:T(1024)(128)(4,1)S(1)} %broadcast_compare_fusion, f32[2,32768]{1,0:T(2,128)S(1)} %all_gather.7), kind=kLoop, calls=%fused_computation.11 | loop fusion | flops 458748 | bytes 950288 | tf_op jit(solution)/shard_map/reduce_sum | solution.py:14
  126.0 12.3 %all-reduce.1 = (f32[2]{0:T(128)S(1)}, f32[2]{0:T(128)S(1)}, f32[]{:T(128)}) all-reduce(f32[2]{0:T(128)S(1)} %get-tuple-element.21, f32[2]{0:T(128)S(1)} %get-tuple-element.15, f32[]{:T(128)} %multiply_reduce_fusion.4), channel_id=1, replica_groups=mesh['row'=4,'col'=8] {'row'}, use_global_device_ids=true, to_apply=%region_13.14 | all-reduce | flops 5 | bytes 40 | tf_op jit(solution)/shard_map/psum | solution.py:120
  139.1 0.6 copy.15
  139.8 0.6 constant_dynamic-slice_fusion
  140.4 0.6 constant_dynamic-slice_fusion.1
  (18 shorter events, 0.1 us)
Async XLA Ops:
  7.2 24.4 %copy-start.7 = (s32[1,1,16]{2,1,0:T(1,128)S(1)}, s32[1,1,16]{2,1,0:T(1,128)}, u32[]{:S(2)}) copy-start(s32[1,1,16]{2,1,0:T(1,128)} %param.14) | copy-start | bytes 196
  7.2 25.6 %copy-start.6 = (f32[2,4096]{1,0:T(2,128)S(1)}, f32[2,4096]{1,0:T(2,128)}, u32[]{:S(2)}) copy-start(f32[2,4096]{1,0:T(2,128)} %param.16) | copy-start | bytes 98308
  7.2 60.7 %all-reduce.7.cloned.1.call-start = ((), (), s32[]{:S(2)}) async-start(), calls=%async_computation.1 | async-start | bytes 262144 | tf_op jit(solution)/shard_map/psum | solution.py:116
  19.8 44.3 %copy-start.8 = (s32[1,1,16]{2,1,0:T(1,128)S(1)}, s32[1,1,16]{2,1,0:T(1,128)}, u32[]{:S(2)}) copy-start(s32[1,1,16]{2,1,0:T(1,128)} %param.13) | copy-start | bytes 196
  19.8 45.7 %copy-start.3 = (s32[16384]{0:T(1024)S(1)}, s32[16384]{0:T(1024)}, u32[]{:S(2)}) copy-start(s32[16384]{0:T(1024)} %param.23) | copy-start | bytes 196612
  19.9 45.8 %copy-start.1 = (f32[16384]{0:T(1024)S(1)}, f32[16384]{0:T(1024)}, u32[]{:S(2)}) copy-start(f32[16384]{0:T(1024)} %param.20) | copy-start | bytes 196612
  19.9 46.4 %copy-start.2 = (s32[32768]{0:T(1024)S(1)}, s32[32768]{0:T(1024)}, u32[]{:S(2)}) copy-start(s32[32768]{0:T(1024)} %param.19) | copy-start | bytes 393220
  19.9 46.4 %copy-start = (f32[32768]{0:T(1024)S(1)}, f32[32768]{0:T(1024)}, u32[]{:S(2)}) copy-start(f32[32768]{0:T(1024)} %param.18) | copy-start | bytes 393220
  19.9 48.0 %copy-start.4 = (f32[16384]{0:T(1024)S(1)}, f32[16384]{0:T(1024)}, u32[]{:S(2)}) copy-start(f32[16384]{0:T(1024)} %param.22) | copy-start | bytes 196612
  19.9 48.0 %copy-start.5 = (f32[16384]{0:T(1024)S(1)}, f32[16384]{0:T(1024)}, u32[]{:S(2)}) copy-start(f32[16384]{0:T(1024)} %param.21) | copy-start | bytes 196612
  32.7 91.8 %all-reduce.5.cloned.1.call-start = ((), (), s32[]{:S(2)}) async-start(), calls=%async_computation | async-start | bytes 524288 | tf_op jit(solution)/shard_map/psum | solution.py:115
Sparse Core Ops, SparseCore 0:
  32.8 35.0 all-reduce.6
  71.0 53.5 all-reduce.4
where the time goes:
time: 148 us
  blocking collectives  49.8 us (34%)
  waiting for transfers between devices  43 us (29%)
  matrix products  30.9 us (21%)
  between operations  16.3 us (11%)
  other arithmetic  4.29 us (3%)
  local copies, waits for them, and re-layouts  3.58 us (2%)
    psum x1, waiting for transfers between devices, on_device(): product = lax.psum(product_part, 'col')  41.9 us
    dot_general x1, matrix products, on_device(): jnp.einsum('tij,stj->tsi', own_tiles, primal_pick, precision=HIGHEST_PREC...  17.2 us
    all_gather x1, blocking collectives, on_device(): primal_group = lax.all_gather(primal_iter, 'row', axis=1, tiled=True)  13.9 us
    psum x1, blocking collectives, on_device(): lax.psum((dual_square, objective_square, objective_dot, bound_sum), 'col')  12.5 us
    psum x1, blocking collectives, on_device(): lax.psum((primal_square, require_square, require_dot), 'row')  12.3 us
    dot_general x1, matrix products, on_device(): jnp.einsum('tij,sti->tsj', own_tiles, dual_pick, precision=HIGHEST_PRECIS...  11.6 us
    all_gather x1, blocking collectives, on_device(): dual_group = lax.all_gather(dual_iter, 'col', axis=1, tiled=True)  11 us
  transfers between devices with their start and end apart: 2, of which 2 were waited for; matrix products, arithmetic and copies ran while one was open for 15% of the time, Pallas kernels for 0%

commit v1 on v0

--- a/solution.py
+++ b/solution.py
@@ -112,7 +112,8 @@
     transposed_part = jnp.einsum(
         "tc,tsj->scj", column_pick, tile_transposed, precision=HIGHEST_PRECISION
     ).reshape(candidates, column_blocks * block_size)
-    product = lax.psum(product_part, "col")
+    pieces = lax.all_gather(product_part, "col")
+    product = jnp.sum(pieces, axis=0)
     transposed = lax.psum(transposed_part, "row")
     primal_full, primal_square, require_square, require_dot = primal_side(
         product, requirement, constraint_kind, dual_group

time: 148 us -> 120 us (0.81)
  waiting for transfers between devices: 43 us -> 11.4 us
  other arithmetic: 4.29 us -> 5.87 us
    psum x1 -> x0, waiting for transfers between devices: 41.9 us -> none  [on_device(): product = lax.psum(product_part, 'col')]
    all_gather x0 -> x1, waiting for transfers between devices: none -> 10.6 us  [on_device(): pieces = lax.all_gather(product_part, 'col')]
    reduce_sum x0 -> x1, other arithmetic: none -> 2.36 us  [on_device(): product = jnp.sum(pieces, axis=0)]
  transfers between devices with their start and end apart: 2 -> 2, of which waited for: 2 -> 2; matrix products, arithmetic and copies ran while one was open for 15% -> 19% of each run, Pallas kernels for 0% -> 0%
where the time goes in v1:
time: 120 us; the launch traced here: 119 us
  blocking collectives  49.7 us (41%)
  matrix products  30.9 us (26%)
  between operations  17.7 us (15%)
  waiting for transfers between devices  11.4 us (10%)
  other arithmetic  5.87 us (5%)
  local copies, waits for them, and re-layouts  3.64 us (3%)
    dot_general x1, matrix products, on_device(): jnp.einsum('tij,stj->tsi', own_tiles, primal_pick, precision=HIGHEST_PREC...  17.2 us
    all_gather x1, blocking collectives, on_device(): primal_group = lax.all_gather(primal_iter, 'row', axis=1, tiled=True)  13.9 us
    psum x1, blocking collectives, on_device(): lax.psum((dual_square, objective_square, objective_dot, bound_sum), 'col')  12.5 us
    psum x1, blocking collectives, on_device(): lax.psum((primal_square, require_square, require_dot), 'row')  12.3 us
    dot_general x1, matrix products, on_device(): jnp.einsum('tij,sti->tsj', own_tiles, dual_pick, precision=HIGHEST_PRECIS...  11.6 us
    all_gather x1, blocking collectives, on_device(): dual_group = lax.all_gather(dual_iter, 'col', axis=1, tiled=True)  11 us
    all_gather x1, waiting for transfers between devices, on_device(): pieces = lax.all_gather(product_part, 'col')  10.6 us
  transfers between devices with their start and end apart: 2, of which 2 were waited for; matrix products, arithmetic and copies ran while one was open for 19% of the time, Pallas kernels for 0%

profile of v1, /device:TPU:0, one launch (start us, length us, event | category | flops | bytes accessed | tf_op | source)
XLA Modules:
  0.0 119.4 jit_solution(16442229243700933055)
XLA Ops:
  8.0 0.0 all-reduce.4.cloned.1.call-start
  8.7 11.0 %all_gather.11 = f32[2,32768]{1,0:T(2,128)S(1)} all-gather(f32[2,4096]{1,0:T(2,128)} %param.17), channel_id=1, replica_groups=mesh['row'=4,'col'=8] {'col'}, dimensions={1}, use_global_device_ids=true | all-gather | bytes 294912 | tf_op jit(solution)/shard_map/all_gather | solution.py:80
  19.7 0.9 fusion.4
  20.7 0.0 copy-start.8
  20.7 0.0 copy-start.1
  20.7 0.0 copy-start
  20.7 0.0 copy-start.3
  20.7 0.0 copy-start.4
  20.7 0.0 copy-start.5
  20.8 11.6 %fusion = f32[16,2,512]{2,1,0:T(2,128)S(1)} fusion(f32[1,1,16,512,512]{4,3,2,1,0:T(8,128)} %param.12, f32[16,2,512]{2,0,1:T(8,128)S(1)} %fusion.4), kind=kOutput, calls=%fused_computation | convolution fusion | flops 100663296 | bytes 16908288 | tf_op jit(solution)/shard_map/tij,sti->tsj/dot_general | solution.py:104
  32.4 0.4 convolution_bitcast_fusion.1
  32.8 0.8 copy.23
  33.5 0.0 all-reduce.4.cloned.1.call-update
  33.6 0.0 all-gather.2.cloned.1.call-start
  33.6 13.9 %all_gather.9 = f32[2,16384]{1,0:T(2,128)S(1)} all-gather(f32[2,4096]{1,0:T(2,128)S(1)} %copy-done.6), channel_id=1, replica_groups=mesh['row'=4,'col'=8] {'row'}, dimensions={1}, use_global_device_ids=true | all-gather | bytes 163840 | tf_op jit(solution)/shard_map/all_gather | solution.py:79
  47.5 0.3 fusion.7
  47.8 17.2 %fusion.2 = f32[16,2,512]{2,1,0:T(2,128)S(1)} fusion(f32[1,1,16,512,512]{4,3,2,1,0:T(8,128)} %param.12, f32[16,2,512]{2,0,1:T(8,128)S(1)} %fusion.7), kind=kOutput, calls=%fused_computation.2 | convolution fusion | flops 100663296 | bytes 16908288 | tf_op jit(solution)/shard_map/tij,stj->tsi/dot_general | solution.py:103
  65.0 0.5 convolution_bitcast_fusion
  65.5 0.9 all_gather_reshape.3
  66.4 0.0 all-gather.2.cloned.1.call-update
  66.5 0.6 multiply_reduce_fusion.5
  67.1 0.6 multiply_reduce_fusion.4
  67.8 0.8 all-reduce.4.cloned.1.call-done
  68.7 1.5 %add_reduce_fusion = (f32[2]{0:T(128)S(1)}, f32[2]{0:T(128)S(1)}, f32[2]{0:T(128)S(1)}, f32[2,16384]{1,0:T(2,128)S(1)}) fusion(f32[16384]{0:T(1024)S(1)} %copy-done.4, f32[16384]{0:T(1024)S(1)} %copy-done.5, pred[16384]{0:T(1024)(128)(4,1)S(1)} %get-tuple-element.26, f32[2,16384]{1,0:T(2,128)} %all-reduce.4.cloned.1.call-done, f32[16384]{0:T(1024)S(1)} %copy-done.1, ...), kind=kLoop, calls=%fused_computation.15 | loop fusion | flops 557050 | bytes 622616 | tf_op jit(solution)/shard_map/reduce_sum | solution.py:28
  70.1 12.5 %all-reduce = (f32[2]{0:T(128)S(1)}, f32[2]{0:T(128)S(1)}, f32[2]{0:T(128)S(1)}, f32[]{:T(128)}) all-reduce(f32[2]{0:T(128)S(1)} %get-tuple-element.10, f32[2]{0:T(128)S(1)} %get-tuple-element.9, f32[2]{0:T(128)S(1)} %get-tuple-element.22, f32[]{:T(128)} %multiply_reduce_fusion.5), channel_id=1, replica_groups=mesh['row'=4,'col'=8] {'col'}, use_global_device_ids=true, to_apply=%region_11.12 | all-reduce | flops 7 | bytes 56 | tf_op jit(solution)/shard_map/psum | solution.py:127
  83.3 0.6 constant_dynamic-slice_fusion
  84.0 10.6 %all-gather.2.cloned.1.call-done = f32[8,2,32768]{2,1,0:T(2,128)} async-done(((f32[1,2,32768]{2,1,0:T(2,128)}), f32[8,2,32768]{2,1,0:T(2,128)}) %all-gather.2.cloned.1.call-update) | async-done | bytes 2097168 | tf_op jit(solution)/shard_map/all_gather | solution.py:115
  94.5 2.4 %reduce_sum.72 = f32[2,32768]{1,0:T(2,128)S(1)} reduce(f32[8,2,32768]{2,1,0:T(2,128)} %all-gather.2.cloned.1.call-done, f32[]{:T(128)} %constant.12.clone.1), dimensions={0}, to_apply=%region_0.0 | reduce | flops 458752 | bytes 2359300 | tf_op jit(solution)/shard_map/reduce_sum | solution.py:116
  96.9 0.7 multiply_reduce_fusion.1
  97.6 12.3 %all-reduce.1 = (f32[2]{0:T(128)S(1)}, f32[2]{0:T(128)S(1)}, f32[]{:T(128)}) all-reduce(f32[2]{0:T(128)S(1)} %get-tuple-element.24, f32[2]{0:T(128)S(1)} %get-tuple-element.18, f32[]{:T(128)} %multiply_reduce_fusion.4), channel_id=1, replica_groups=mesh['row'=4,'col'=8] {'row'}, use_global_device_ids=true, to_apply=%region_13.14 | all-reduce | flops 5 | bytes 40 | tf_op jit(solution)/shard_map/psum | solution.py:121
  110.7 0.6 copy.16
  111.3 0.6 constant_dynamic-slice_fusion.1
  (19 shorter events, 0.1 us)
Async XLA Ops:
  8.0 24.4 %copy-start.7 = (s32[1,1,16]{2,1,0:T(1,128)S(1)}, s32[1,1,16]{2,1,0:T(1,128)}, u32[]{:S(2)}) copy-start(s32[1,1,16]{2,1,0:T(1,128)} %param.14) | copy-start | bytes 196
  8.0 25.6 %copy-start.6 = (f32[2,4096]{1,0:T(2,128)S(1)}, f32[2,4096]{1,0:T(2,128)}, u32[]{:S(2)}) copy-start(f32[2,4096]{1,0:T(2,128)} %param.16) | copy-start | bytes 98308
  8.0 60.6 %all-reduce.4.cloned.1.call-start = ((), (), s32[]{:S(2)}) async-start(), calls=%async_computation.1 | async-start | bytes 262144 | tf_op jit(solution)/shard_map/psum | solution.py:117
  20.7 44.3 %copy-start.8 = (s32[1,1,16]{2,1,0:T(1,128)S(1)}, s32[1,1,16]{2,1,0:T(1,128)}, u32[]{:S(2)}) copy-start(s32[1,1,16]{2,1,0:T(1,128)} %param.13) | copy-start | bytes 196
  20.7 45.8 %copy-start.1 = (f32[16384]{0:T(1024)S(1)}, f32[16384]{0:T(1024)}, u32[]{:S(2)}) copy-start(f32[16384]{0:T(1024)} %param.20) | copy-start | bytes 196612
  20.7 46.4 %copy-start = (f32[32768]{0:T(1024)S(1)}, f32[32768]{0:T(1024)}, u32[]{:S(2)}) copy-start(f32[32768]{0:T(1024)} %param.18) | copy-start | bytes 393220
  20.7 47.0 %copy-start.3 = (s32[16384]{0:T(1024)S(1)}, s32[16384]{0:T(1024)}, u32[]{:S(2)}) copy-start(s32[16384]{0:T(1024)} %param.23) | copy-start | bytes 196612
  20.7 47.1 %copy-start.2 = (s32[32768]{0:T(1024)S(1)}, s32[32768]{0:T(1024)}, u32[]{:S(2)}) copy-start(s32[32768]{0:T(1024)} %param.19) | copy-start | bytes 393220
  20.7 47.9 %copy-start.4 = (f32[16384]{0:T(1024)S(1)}, f32[16384]{0:T(1024)}, u32[]{:S(2)}) copy-start(f32[16384]{0:T(1024)} %param.22) | copy-start | bytes 196612
  20.7 47.9 %copy-start.5 = (f32[16384]{0:T(1024)S(1)}, f32[16384]{0:T(1024)}, u32[]{:S(2)}) copy-start(f32[16384]{0:T(1024)} %param.21) | copy-start | bytes 196612
  33.6 61.0 %all-gather.2.cloned.1.call-start = ((), (), s32[]{:S(2)}) async-start(), calls=%async_computation | async-start | bytes 2359296 | tf_op jit(solution)/shard_map/all_gather | solution.py:115
Sparse Core Ops, SparseCore 0:
  33.7 34.9 all-reduce.3
Sparse Core Ops, SparseCore 1:
  66.6 27.9 all-gather.1
